TPU v7x, 32 devices: a whole 2x2x4 slice. The times are simulated.
32 devices in a mesh: slab: 32 (over z, y, x, core).
Axes of the slice: x: 2, y: 2, z: 4, core: 2. Of those that a mesh axis runs over, the one named last changes fastest.
Arguments:
- krylov_basis_block: float32 [16, 256, 16, 128], P(None, 'slab'), may hold values from -6 to 6
- companion: float32 [16, 256, 16, 128], P(None, 'slab'), may hold values from -6 to 6
- region: int32 [256, 16, 128], P('slab'), may hold values from 0 to 7
- inv_density: float32 [8], replicated, may hold values from 0.3 to 3
- stiffness: float32 [8], replicated, may hold values from 0.5 to 3
- damping: float32 [8], replicated, may hold values from 0.5 to 4
Outputs:
- new_block: float32 [16, 256, 16, 128], P(None, 'slab')
- projection: float32 [16, 16], replicated
- rfactor: float32 [16, 16], replicated
All inputs are finite; a program needn't handle non-finite values.
Results may differ from a plain program's by a relative error of at most 0.00012.
Values sent between devices are 32-bit elements; how exact they have to be, the bound alone decides.
A program may use at most 64 MiB of HBM per device.

v0:
```python
import jax
import jax.numpy as jnp
from jax import lax
from jax.sharding import PartitionSpec as P


def extended(cells, sides, width):
    for axis, dim in sides:
        count = lax.axis_size(axis)
        ends = count - 1
        head = lax.slice_in_dim(cells, 0, width, axis=dim)
        tail = lax.slice_in_dim(cells, cells.shape[dim] - width, cells.shape[dim], axis=dim)
        cells = jnp.concatenate(
            [
                lax.ppermute(tail, axis, [(i, (i + 1) % count) for i in range(ends)]),
                cells,
                lax.ppermute(head, axis, [((i + 1) % count, i) for i in range(ends)]),
            ],
            axis=dim,
        )
    return cells


def lookup(region, table):
    picks = region[None] == jnp.arange(table.shape[0], dtype=jnp.int32)[:, None, None, None]
    return jnp.sum(jnp.where(picks, table[:, None, None, None], jnp.float32(0.0)), axis=0)


def operate(operator_applied, cx, mass, damp, companion):
    padded_basis = jnp.pad(operator_applied, ((0, 0), (0, 0), (1, 1), (1, 1)))
    cpad = jnp.pad(cx, ((0, 0), (1, 1), (1, 1)), mode="edge")
    center_coefficient = padded_basis[:, 1:-1, 1:-1, 1:-1]
    ccenter = cpad[1:-1, 1:-1, 1:-1]
    total = -mass * center_coefficient + damp * companion
    shifts = [
        (slice(2, None), slice(1, -1), slice(1, -1)),
        (slice(0, -2), slice(1, -1), slice(1, -1)),
        (slice(1, -1), slice(2, None), slice(1, -1)),
        (slice(1, -1), slice(0, -2), slice(1, -1)),
        (slice(1, -1), slice(1, -1), slice(2, None)),
        (slice(1, -1), slice(1, -1), slice(0, -2)),
    ]
    for selection_mask in shifts:
        neighbour_coefficient = padded_basis[
            :, selection_mask[0], selection_mask[1], selection_mask[2]
        ]
        bond = 0.5 * (ccenter + cpad[selection_mask])
        total = total + bond * (center_coefficient - neighbour_coefficient)
    return total


def block_products(left, right):
    return jnp.dot(left, right.T, precision=lax.Precision.HIGHEST)


def shards(krylov_basis_block, companion, region, inv_density, stiffness, damping):
    block_width = krylov_basis_block.shape[0]
    coef = lookup(region, inv_density)
    mass = lookup(region, stiffness)
    damp = lookup(region, damping)
    stacked = jnp.concatenate([krylov_basis_block, coef[None]], axis=0)
    padded = extended(stacked, (("slab", 1),), 1)
    operator_applied = padded[:block_width]
    cplanes = padded[block_width]
    first_plane = jnp.where(cplanes[0] > 0.0, cplanes[0], coef[0])
    last_plane = jnp.where(cplanes[-1] > 0.0, cplanes[-1], coef[-1])
    cx = jnp.concatenate([first_plane[None], coef, last_plane[None]], axis=0)
    fresh = operate(operator_applied, cx, mass, damp, companion)
    cell_count = (
        krylov_basis_block.shape[1]
        * krylov_basis_block.shape[2]
        * krylov_basis_block.shape[3]
        * lax.axis_size("slab")
    )
    basis_matrix = krylov_basis_block.reshape(block_width, -1)
    image_matrix = fresh.reshape(block_width, -1)
    projection, fresh_gram, basis_gram = lax.psum(
        (
            block_products(basis_matrix, image_matrix) / cell_count,
            block_products(image_matrix, image_matrix) / cell_count,
            block_products(basis_matrix, basis_matrix) / cell_count,
        ),
        "slab",
    )
    cross = block_products(projection.T, projection.T)
    spread = jnp.dot(
        projection.T,
        jnp.dot(basis_gram, projection, precision=lax.Precision.HIGHEST),
        precision=lax.Precision.HIGHEST,
    )
    gram = fresh_gram - 2.0 * cross + spread
    lower = jnp.linalg.cholesky(gram)
    reduced_products = image_matrix - jnp.dot(
        projection.T, basis_matrix, precision=lax.Precision.HIGHEST
    )
    new_block = lax.linalg.triangular_solve(lower, reduced_products, left_side=True, lower=True)
    return (new_block.reshape(krylov_basis_block.shape), projection, lower.T)


def solution(mesh):
    placed = (
        P(None, "slab", None, None),
        P(None, "slab", None, None),
        P("slab", None, None),
        P(),
        P(),
        P(),
    )
    return jax.shard_map(
        shards,
        mesh=mesh,
        in_specs=placed,
        out_specs=(P(None, "slab", None, None), P(), P()),
        check_vma=False,
    )
```

profile of v0, /device:TPU:0, one launch (start us, length us, event | category | flops | bytes accessed | tf_op | source)
XLA Modules:
  0.0 75.6 jit_solution(6152154537756962666)
XLA Ops:
  0.6 0.0 copy-start
  0.6 1.2 %select_reduce_fusion.2 = (f32[8,16,128]{2,1,0:T(8,128)S(1)}, f32[8,16,128]{2,1,0:T(8,128)S(1)}, f32[8,16,128]{2,1,0:T(8,128)S(1)}) fusion(f32[8]{0:T(128)} %param.10, s32[8,16,128]{2,1,0:T(8,128)} %param.8, f32[8]{0:T(128)} %param.9, f32[8]{0:T(128)} %param.11), kind=kLoop, calls=%fused_computation.54 | loop fusion | flops 868352 | bytes 262240 | tf_op jit(solution)/shard_map/reduce_sum | solution.py:26
  1.8 1.0 %pad_maximum_fusion.4 = (f32[17,1,16,128]{3,2,1,0:T(8,128)S(1)}, f32[17,1,16,128]{3,2,1,0:T(8,128)S(1)}) fusion(f32[1,8,16,128]{3,2,1,0:T(8,128)S(1)} %bitcast.65, f32[16,8,16,128]{3,2,1,0:T(8,128)} %param.6), kind=kLoop, calls=%fused_computation.56 | loop fusion | flops 69632 | bytes 1392640 | tf_op jit(solution)/shard_map/concatenate | solution.py:61
  2.8 1.3 %collective-permute-start = (f32[17,1,16,128]{3,2,1,0:T(8,128)S(1)}, f32[17,1,16,128]{3,2,1,0:T(8,128)S(1)}, u32[]{:S(2)}, u32[]{:S(2)}) collective-permute-start(f32[17,1,16,128]{3,2,1,0:T(8,128)S(1)} %get-tuple-element.16), channel_id=1, source_target_pairs={{1,0},{2,1},{3,2},{4,3},{5,4},{6,5},{7,6},{8,7},{9,8},{10,9},{11,1... | collective-permute-start | bytes 417800 | tf_op jit(solution)/shard_map/ppermute | solution.py:17
  4.1 3.0 %collective-permute-start.1 = (f32[17,1,16,128]{3,2,1,0:T(8,128)S(1)}, f32[17,1,16,128]{3,2,1,0:T(8,128)S(1)}, u32[]{:S(2)}, u32[]{:S(2)}) collective-permute-start(f32[17,1,16,128]{3,2,1,0:T(8,128)S(1)} %get-tuple-element.15), channel_id=1, source_target_pairs={{0,1},{1,2},{2,3},{3,4},{4,5},{5,6},{6,7},{7,8},{8,9},{9,10},{10,1... | collective-permute-start | bytes 417800 | tf_op jit(solution)/shard_map/ppermute | solution.py:15
  7.2 0.0 copy-start.1
  7.2 4.0 %fusion.4 = f32[16,16]{0,1:T(8,128)S(1)} fusion(f32[16,8,16,128]{3,2,1,0:T(8,128)} %param.6), kind=kOutput, calls=%fused_computation.14 | convolution fusion | flops 50331904 | bytes 1049600 | tf_op jit(solution)/shard_map/dot_general | solution.py:53
  11.1 0.0 collective-permute-done
  11.2 0.0 collective-permute-done.1
  11.3 0.1 fusion.46
  11.3 0.1 fusion.34
  11.5 0.0 copy-done
  11.5 3.3 %select_maximum_fusion = f32[16,10,18,130]{3,2,1,0:T(8,128)S(1)} fusion(f32[17,1,16,128]{3,2,1,0:T(8,128)S(1)} %collective-permute-done, f32[17,1,16,128]{3,2,1,0:T(8,128)S(1)} %collective-permute-done.1, f32[1,8,16,128]{3,2,1,0:T(8,128)S(1)} %bitcast.66, f32[16,8,16,128]{3,2,1,0:T(8,128)S(1)} %copy-done), kind=kLoop, calls=%fused_computation.5 | loop fusion | flops 6739200 | bytes 2890240 | tf_op jit(solution)/shard_map/concatenate | solution.py:13
  14.8 0.0 copy-done.1
  14.8 1.2 %fusion.12 = f32[16,8,16,128]{3,2,1,0:T(8,128)S(1)} fusion(f32[16,8,16,128]{3,2,1,0:T(8,128)S(1)} %copy-done, f32[16,10,18,130]{3,2,1,0:T(8,128)S(1)} %select_maximum_fusion, f32[17,1,16,128]{3,2,1,0:T(8,128)S(1)} %collective-permute-done.1, f32[1,8,16,128]{3,2,1,0:T(8,128)S(1)} %bitcast.67, f32[17,1,16,128]{3,2,1,0:T(8,128)S(1)} %collective-permute-done, ...), kind=kLoop, calls=%fused_computation.26 | loop fusion | flops 6553600 | bytes 8208384 | tf_op jit(solution)/shard_map/add | solution.py:48
  16.0 2.3 %fusion.7 = f32[16,16]{1,0:T(8,128)S(1)} fusion(f32[16,8,16,128]{3,2,1,0:T(8,128)S(1)} %copy-done, f32[16,8,16,128]{3,2,1,0:T(8,128)S(1)} %fusion.12), kind=kOutput, calls=%fused_computation.19 | convolution fusion | flops 50331904 | bytes 2098176 | tf_op jit(solution)/shard_map/dot_general | solution.py:53
  18.4 1.9 %fusion.8 = f32[16,16]{0,1:T(8,128)S(1)} fusion(f32[16,8,16,128]{3,2,1,0:T(8,128)S(1)} %fusion.12), kind=kOutput, calls=%fused_computation.21 | convolution fusion | flops 50331904 | bytes 1049600 | tf_op jit(solution)/shard_map/dot_general | solution.py:53
  20.2 44.9 %all-reduce.1 = (f32[16,16]{1,0:T(8,128)S(1)}, f32[16,16]{0,1:T(8,128)S(1)}, f32[16,16]{0,1:T(8,128)S(1)}) all-reduce(f32[16,16]{1,0:T(8,128)S(1)} %fusion.7, f32[16,16]{0,1:T(8,128)S(1)} %fusion.8, f32[16,16]{0,1:T(8,128)S(1)} %fusion.4), channel_id=1, replica_groups=mesh['slab'=32] {'slab'}, use_global_device_ids=true, to_apply=%region_4.5 | all-reduce | flops 768 | bytes 6144 | tf_op jit(solution)/shard_map/psum | solution.py:77
  65.2 0.0 copy-start.2
  65.2 0.2 fusion.47
  65.4 0.2 fusion.5
  65.6 0.2 convolution_add_fusion
  65.8 0.1 copy.30
  65.8 1.5 %cholesky.16 = f32[16,16]{1,0:T(8,128)S(1)} custom-call(f32[16,16]{1,0:T(8,128)S(1)} %fusion.44), custom_call_target="Cholesky" | custom-call | tf_op jit(solution)/shard_map/jit(cholesky)/cholesky | solution.py:92
  67.3 0.6 compare_reduce_fusion
  68.0 0.6 fusion.45
  68.6 1.2 %custom-call.6 = f32[1,16,16]{1,2,0:T(8,128)S(1)} custom-call(f32[1,16,16]{2,1,0:T(8,128)S(1)} %get-tuple-element.30), custom_call_target="InvertDiagBlocksLowerTriangular" | custom-call | tf_op jit(solution)/shard_map/triangular_solve | solution.py:96
  69.9 2.0 %fusion.3 = f32[2,8,128,128]{3,1,2,0:T(8,128)S(1)} fusion(f32[16,16]{1,0:T(8,128)S(1)} %get-tuple-element.12, f32[2,8,128,128]{3,2,1,0:T(8,128)S(1)} %bitcast.63, f32[2,8,128,128]{3,2,1,0:T(8,128)S(1)} %bitcast.64), kind=kOutput, calls=%fused_computation.11 | convolution fusion | flops 50593792 | bytes 3146752 | tf_op jit(solution)/shard_map/dot_general | solution.py:93
  71.9 0.2 copy.46
  72.1 1.5 %fusion.25 = f32[16,8,16,128]{3,0,2,1:T(8,128)S(1)} fusion(f32[8,16,128,16]{2,1,0,3:T(8,128)S(1)} %bitcast.68, f32[1,16,16]{1,2,0:T(8,128)S(1)} %custom-call.6), kind=kOutput, calls=%fused_computation.46 | convolution fusion | flops 50331648 | bytes 2098176 | tf_op jit(solution)/shard_map/triangular_solve | solution.py:96
  73.6 1.3 %copy.33 = f32[16,8,16,128]{3,2,1,0:T(8,128)} copy(f32[16,8,16,128]{3,0,2,1:T(8,128)S(1)} %fusion.25) | data formatting | bytes 2097152
  74.9 0.0 copy-done.2
  74.9 0.7 copy.34
  (7 shorter events, 0.1 us)
Async XLA Ops:
  0.6 10.9 %copy-start = (f32[16,8,16,128]{3,2,1,0:T(8,128)S(1)}, f32[16,8,16,128]{3,2,1,0:T(8,128)}, u32[]{:S(2)}) copy-start(f32[16,8,16,128]{3,2,1,0:T(8,128)} %param.6) | copy-start | bytes 3145732
  2.8 8.3 %collective-permute-start = (f32[17,1,16,128]{3,2,1,0:T(8,128)S(1)}, f32[17,1,16,128]{3,2,1,0:T(8,128)S(1)}, u32[]{:S(2)}, u32[]{:S(2)}) collective-permute-start(f32[17,1,16,128]{3,2,1,0:T(8,128)S(1)} %get-tuple-element.16), channel_id=1, source_target_pairs={{1,0},{2,1},{3,2},{4,3},{5,4},{6,5},{7,6},{8,7},{9,8},{10,9},{11,1... | collective-permute-start | bytes 417800 | tf_op jit(solution)/shard_map/ppermute | solution.py:17
  4.1 7.0 %collective-permute-start.1 = (f32[17,1,16,128]{3,2,1,0:T(8,128)S(1)}, f32[17,1,16,128]{3,2,1,0:T(8,128)S(1)}, u32[]{:S(2)}, u32[]{:S(2)}) collective-permute-start(f32[17,1,16,128]{3,2,1,0:T(8,128)S(1)} %get-tuple-element.15), channel_id=1, source_target_pairs={{0,1},{1,2},{2,3},{3,4},{4,5},{5,6},{6,7},{7,8},{8,9},{9,10},{10,1... | collective-permute-start | bytes 417800 | tf_op jit(solution)/shard_map/ppermute | solution.py:15
  7.2 7.6 %copy-start.1 = (f32[16,8,16,128]{3,2,1,0:T(8,128)S(1)}, f32[16,8,16,128]{3,2,1,0:T(8,128)}, u32[]{:S(2)}) copy-start(f32[16,8,16,128]{3,2,1,0:T(8,128)} %param.7) | copy-start | bytes 3145732
  65.2 9.7 %copy-start.2 = (f32[16,16]{1,0:T(8,128)}, f32[16,16]{1,0:T(8,128)S(1)}, u32[]{:S(2)}) copy-start(f32[16,16]{1,0:T(8,128)S(1)} %get-tuple-element.12) | copy-start | bytes 3076
where the time goes:
time: 75.9 us; the launch traced here: 75.6 us
  blocking collectives  44.9 us (59%)
  matrix products  12.2 us (16%)
  other arithmetic  10.9 us (14%)
  starting transfers between devices  4.33 us (6%)
  local copies, waits for them, and re-layouts  2.34 us (3%)
  between operations  0.81 us (1%)
    psum x1, blocking collectives, shards(): lax.psum((block_products(basis_matrix, image_matrix) / cell_count, block_...  44.9 us
    dot_general x4, matrix products, block_products(): return jnp.dot(left, right.T, precision=lax.Precision.HIGHEST)  8.35 us
    concatenate x1, other arithmetic, extended(): jnp.concatenate([lax.ppermute(tail, axis, [(i, (i + 1) % count) for i in...  3.29 us
    ppermute x1, starting transfers between devices, extended(): lax.ppermute(tail, axis, [(i, (i + 1) % count) for i in range(ends)])  3.04 us
    unnamed x9, local copies, waits for them, and re-layouts  2.18 us
    another operation x3, other arithmetic, shards(): lower = jnp.linalg.cholesky(gram)  2.14 us
    dot_general x1, matrix products, shards(): jnp.dot(projection.T, basis_matrix, precision=lax.Precision.HIGHEST)  2 us
  transfers between devices with their start and end apart: 2, of which 0 were waited for; matrix products, arithmetic and copies ran while one was open for 5% of the time, Pallas kernels for 0%

commit v1 on v0

v1 whole, which is shorter than its diff:
```python
import functools

import jax
import jax.numpy as jnp
from jax import lax
from jax.experimental import pallas as pl
from jax.experimental.pallas import tpu as pltpu
from jax.sharding import PartitionSpec as P

AXIS = "slab"
MESH = pl.DeviceIdType.MESH
F32, BF16 = jnp.float32, jnp.bfloat16


def radices(count):
    out = []
    while count > 1:
        for r in (8, 4, 2):
            if count % r == 0:
                break
        else:
            r = next(q for q in range(3, count + 1) if count % q == 0)
        out.append(r)
        count //= r
    return out


def split3(a):
    p = a.astype(BF16)
    rest = a - p.astype(F32)
    q = rest.astype(BF16)
    return p, q, (rest - q.astype(F32)).astype(BF16)


def step_kernel(
    n, planes, ny, cells,
    b_hbm, c_hbm, reg_hbm, dens, stiff, dampt,
    out_hbm, proj_ref, rfac_ref,
    bv, cv, reg, coef, co, s, acc, ov, *rest,
):
    rads = radices(n)
    slots = rest[: len(rads)]
    load_sem, halo_send, halo_recv, reg_send, reg_recv, out_sem = rest[len(rads): len(rads) + 6]
    ph_send = rest[len(rads) + 6: 2 * len(rads) + 6]
    ph_recv = rest[2 * len(rads) + 6:]
    k = b_hbm.shape[0]
    rows = planes * ny
    span = rows + 2 * ny
    nz = b_hbm.shape[-1]
    tables = dens.shape[0]
    me = lax.axis_index(AXIS)
    has_left, has_right = me > 0, me < n - 1
    left, right = lax.rem(me + n - 1, n), lax.rem(me + 1, n)

    digits, stride = [], 1
    for r in rads:
        digits.append((stride, lax.rem(me // stride, r)))
        stride *= r

    def peer(ph, o):
        st, d = digits[ph]
        pd = lax.rem(d + o, rads[ph])
        return me + (pd - d) * st, pd

    barrier = pltpu.get_barrier_semaphore()

    @pl.when(has_left)
    def _():
        pl.semaphore_signal(barrier, inc=1, device_id=(left,), device_id_type=MESH)

    @pl.when(has_right)
    def _():
        pl.semaphore_signal(barrier, inc=1, device_id=(right,), device_id_type=MESH)

    for ph, r in enumerate(rads):
        for o in range(1, r):
            pl.semaphore_signal(barrier, inc=1, device_id=(peer(ph, o)[0],), device_id_type=MESH)

    bv3 = bv.reshape(k, span, nz)
    cp_r = pltpu.make_async_copy(reg_hbm, reg.at[pl.ds(1, planes)], load_sem.at[0])
    cp_b = pltpu.make_async_copy(b_hbm, bv3.at[:, pl.ds(ny, rows), :], load_sem.at[1])
    cp_c = pltpu.make_async_copy(c_hbm, cv.reshape(k, rows, nz), load_sem.at[2])
    cp_r.start()
    cp_b.start()
    cp_c.start()

    pl.semaphore_wait(
        barrier, sum(r - 1 for r in rads) + has_left.astype(jnp.int32) + has_right.astype(jnp.int32)
    )

    def halo(up):
        i = 0 if up else 1
        src = pl.ds(rows - ny, ny) if up else pl.ds(0, ny)
        dst = pl.ds(0, ny) if up else pl.ds(rows + ny, ny)
        to = right if up else left
        rc = pltpu.make_async_remote_copy(
            src_ref=reg_hbm.at[planes - 1 if up else 0], dst_ref=reg.at[0 if up else planes + 1],
            send_sem=reg_send.at[i], recv_sem=reg_recv.at[i],
            device_id=(to,), device_id_type=MESH)
        vc = pltpu.make_async_remote_copy(
            src_ref=b_hbm.at[:, src, :], dst_ref=bv3.at[:, dst, :],
            send_sem=halo_send.at[i], recv_sem=halo_recv.at[i],
            device_id=(to,), device_id_type=MESH)
        return rc, vc

    @pl.when(has_right)
    def _():
        for c in halo(True):
            c.start()

    @pl.when(has_left)
    def _():
        for c in halo(False):
            c.start()

    def lookup(r, table):
        out = jnp.zeros(r.shape, F32)
        for t in range(tables):
            out = jnp.where(r == t, table[t], out)
        return out

    cp_r.wait()
    coef[pl.ds(1, planes)] = lookup(reg[pl.ds(1, planes)], dens)
    cp_b.wait()
    cp_c.wait()

    lane = lax.broadcasted_iota(jnp.int32, (ny, nz), 1)
    acc[...] = jnp.zeros(acc.shape, F32)

    def plane(x):
        c = coef[x + 1]
        r = reg[x + 1]
        cxm, cxp = coef[x], coef[x + 2]
        cym = jnp.concatenate([c[:1], c[:-1]], axis=0)
        cyp = jnp.concatenate([c[1:], c[-1:]], axis=0)
        czm = jnp.where(lane == 0, c, pltpu.roll(c, 1, 1))
        czp = jnp.where(lane == nz - 1, c, pltpu.roll(c, nz - 1, 1))
        bonds = [0.5 * (c + d) for d in (cxm, cxp, cym, cyp, czm, czp)]
        co[0] = bonds[0] + bonds[1] + bonds[2] + bonds[3] + bonds[4] + bonds[5] - lookup(r, stiff)
        co[1] = lookup(r, dampt)
        for i in range(4):
            co[2 + i] = bonds[i]
        co[6] = jnp.where(lane == 0, 0.0, bonds[4])
        co[7] = jnp.where(lane == nz - 1, 0.0, bonds[5])
        base = (x + 1) * ny

        def at(row):
            return bv[pl.ds(row, k, stride=span), :]

        for y in range(ny):
            w = [jnp.broadcast_to(co[i, pl.ds(y, 1), :], (k, nz)) for i in range(8)]
            v = at(base + y)
            f = w[0] * v + w[1] * cv[pl.ds(x * ny + y, k, stride=rows), :]
            f = f - w[2] * at(base + y - ny) - w[3] * at(base + y + ny)
            if y > 0:
                f = f - w[4] * at(base + y - 1)
            if y < ny - 1:
                f = f - w[5] * at(base + y + 1)
            f = f - w[6] * pltpu.roll(v, 1, 1) - w[7] * pltpu.roll(v, nz - 1, 1)
            for i, (pb, pf) in enumerate(zip(split3(v), split3(f))):
                s[x, pl.ds(2 * k * i, k), pl.ds(y * nz, nz)] = pb
                s[x, pl.ds(2 * k * i + k, k), pl.ds(y * nz, nz)] = pf
        sx = s[x]
        acc[...] += lax.dot_general(sx, sx, (((1,), (1,)), ((), ())), preferred_element_type=F32)

    lax.fori_loop(1, planes - 1, lambda x, _: (plane(x), 0)[1], 0)

    @pl.when(has_left)
    def _():
        for c in halo(True):
            c.wait_recv()
        coef[0] = lookup(reg[0], dens)

    @pl.when(me == 0)
    def _():
        bv3[:, pl.ds(0, ny), :] = jnp.zeros((k, ny, nz), F32)
        coef[0] = coef[1]

    @pl.when(has_right)
    def _():
        for c in halo(False):
            c.wait_recv()
        coef[planes + 1] = lookup(reg[planes + 1], dens)

    @pl.when(me == n - 1)
    def _():
        bv3[:, pl.ds(rows + ny, ny), :] = jnp.zeros((k, ny, nz), F32)
        coef[planes + 1] = coef[planes]

    lax.fori_loop(0, 2, lambda i, _: (plane(i * (planes - 1)), 0)[1], 0)

    g = acc[...]
    g = g[: 2 * k] + g[2 * k: 4 * k] + g[4 * k:]
    g = g[:, : 2 * k] + g[:, 2 * k: 4 * k] + g[:, 4 * k:]
    parts = nz // (2 * k)
    tall = (2 * k) // parts
    packed = jnp.concatenate([g[i * tall: (i + 1) * tall] for i in range(parts)], axis=1)

    for ph, r in enumerate(rads):
        d = digits[ph][1]
        buf = slots[ph]
        buf[d] = packed

        def exchange(to, mine):
            return pltpu.make_async_remote_copy(
                src_ref=buf.at[d], dst_ref=buf.at[mine],
                send_sem=ph_send[ph].at[mine], recv_sem=ph_recv[ph].at[mine],
                device_id=(to,), device_id_type=MESH)

        sent = []
        for o in range(1, r):
            to, pd = peer(ph, o)
            c = pltpu.make_async_remote_copy(
                src_ref=buf.at[d], dst_ref=buf.at[d],
                send_sem=ph_send[ph].at[pd], recv_sem=ph_recv[ph].at[d],
                device_id=(to,), device_id_type=MESH)
            c.start()
            sent.append(c)
        for o in range(1, r):
            to, pd = peer(ph, o)
            exchange(to, pd).wait_recv()
        packed = buf[0]
        for i in range(1, r):
            packed = packed + buf[i]
        for c in sent:
            c.wait_send()

    packed = packed / F32(cells)
    g = jnp.concatenate([packed[:, 2 * k * i: 2 * k * (i + 1)] for i in range(parts)], axis=0)
    bb, p, pt, ff = g[:k, :k], g[:k, k:], g[k:, :k], g[k:, k:]
    dot = functools.partial(jnp.dot, precision=lax.Precision.HIGHEST, preferred_element_type=F32)
    gram = ff - dot(pt, 2.0 * p - dot(bb, p))
    proj_ref[...] = p

    ri = lax.broadcasted_iota(jnp.int32, (k, k), 0)
    ci = lax.broadcasted_iota(jnp.int32, (k, k), 1)
    m = jnp.concatenate([gram, -pt, (ri == ci).astype(F32)], axis=1)
    rid = lax.broadcasted_iota(jnp.int32, (k, 1), 0)
    for i in range(k):
        rs = lax.rsqrt(m[i: i + 1, i: i + 1])
        u = m[i: i + 1, :] * rs
        mult = jnp.where(rid > i, m[:, i: i + 1] * rs, 0.0)
        m = jnp.where(rid == i, u, m - mult * u)
    rfac_ref[...] = jnp.where(ri <= ci, m[:, :k], 0.0)

    w = jnp.concatenate(split3(m[:, k:]), axis=0)
    w = jnp.concatenate([w, w, w], axis=1)

    ov3 = ov.reshape(k, rows, nz)

    def apply(x, _):
        o = jnp.dot(w, s[x], preferred_element_type=F32)
        o = o[:k] + (o[k: 2 * k] + o[2 * k:])
        for y in range(ny):
            ov[pl.ds(x * ny + y, k, stride=rows), :] = o[:, y * nz: (y + 1) * nz]
        part = pl.ds(x * ny, ny)
        pltpu.make_async_copy(ov3.at[:, part, :], out_hbm.at[:, part, :], out_sem.at[x]).start()
        return 0

    lax.fori_loop(0, planes, apply, 0)

    @pl.when(has_right)
    def _():
        for c in halo(True):
            c.wait_send()

    @pl.when(has_left)
    def _():
        for c in halo(False):
            c.wait_send()

    for x in range(planes):
        part = pl.ds(x * ny, ny)
        pltpu.make_async_copy(ov3.at[:, part, :], out_hbm.at[:, part, :], out_sem.at[x]).wait()


def solution(mesh):
    n = mesh.shape[AXIS]
    rads = radices(n)

    def shards(b, c, region, dens, stiff, dampt):
        k, planes, ny, nz = b.shape
        rows = planes * ny
        tall = 2 * k * 2 * k // nz
        hbm = pl.BlockSpec(memory_space=pl.ANY)
        vm = pl.BlockSpec(memory_space=pltpu.VMEM)
        sm = pl.BlockSpec(memory_space=pltpu.SMEM)
        new, proj, rfac = pl.pallas_call(
            functools.partial(step_kernel, n, planes, ny, planes * ny * nz * n),
            out_shape=(
                jax.ShapeDtypeStruct((k, rows, nz), F32),
                jax.ShapeDtypeStruct((k, k), F32),
                jax.ShapeDtypeStruct((k, k), F32),
            ),
            in_specs=[hbm, hbm, hbm, sm, sm, sm],
            out_specs=(hbm, vm, vm),
            scratch_shapes=[
                pltpu.VMEM((k * (rows + 2 * ny), nz), F32),
                pltpu.VMEM((k * rows, nz), F32),
                pltpu.VMEM((planes + 2, ny, nz), jnp.int32),
                pltpu.VMEM((planes + 2, ny, nz), F32),
                pltpu.VMEM((8, ny, nz), F32),
                pltpu.VMEM((planes, 6 * k, ny * nz), BF16),
                pltpu.VMEM((6 * k, 6 * k), F32),
                pltpu.VMEM((k * rows, nz), F32),
            ]
            + [pltpu.VMEM((r, tall, nz), F32) for r in rads]
            + [
                pltpu.SemaphoreType.DMA((3,)),
                pltpu.SemaphoreType.DMA((2,)),
                pltpu.SemaphoreType.DMA((2,)),
                pltpu.SemaphoreType.DMA((2,)),
                pltpu.SemaphoreType.DMA((2,)),
                pltpu.SemaphoreType.DMA((planes,)),
            ]
            + [pltpu.SemaphoreType.DMA((r,)) for r in rads]
            + [pltpu.SemaphoreType.DMA((r,)) for r in rads],
            compiler_params=pltpu.CompilerParams(collective_id=0, has_side_effects=True),
        )(b.reshape(k, rows, nz), c.reshape(k, rows, nz), region, dens, stiff, dampt)
        return new.reshape(b.shape), proj, rfac

    placed = (
        P(None, AXIS, None, None),
        P(None, AXIS, None, None),
        P(AXIS, None, None),
        P(),
        P(),
        P(),
    )
    return jax.shard_map(
        shards,
        mesh=mesh,
        in_specs=placed,
        out_specs=(P(None, AXIS, None, None), P(), P()),
        check_vma=False,
    )
```

time: 75.9 us -> 28.9 us (0.38)
  blocking collectives: 44.9 us -> 0 us
  Pallas kernels: 0 us -> 24.4 us
  matrix products: 12.2 us -> 0 us
  other arithmetic: 10.9 us -> 0 us
  starting transfers between devices: 4.33 us -> 0 us
  local copies, waits for them, and re-layouts: 2.34 us -> 3.6 us
    psum x1 -> x0, blocking collectives: 44.9 us -> none  [shards(): lax.psum((block_products(basis_matrix, image_matrix) / cell_count, block_...]
    pallas_call x0 -> x1, Pallas kernels: none -> 24.4 us  [shards(): pl.pallas_call(functools.partial(step_kernel, n, planes, ny, planes * ny...]
    dot_general x7 -> x0, matrix products: 10.7 us -> none  [the longest x4 8.35 us: block_products(): return jnp.dot(left, right.T, precision=lax.Precision.HIGHEST)]
    ppermute x2 -> x0, starting transfers between devices: 4.33 us -> none  [the longest x1 3.04 us: extended(): lax.ppermute(tail, axis, [(i, (i + 1) % count) for i in range(ends)])]
    concatenate x4 -> x0, other arithmetic: 4.32 us -> none  [the longest x1 3.29 us: extended(): jnp.concatenate([lax.ppermute(tail, axis, [(i, (i + 1) % count) for i in...]
    another operation x4 -> x0, other arithmetic: 3.37 us -> none  [the longest x3 2.14 us: shards(): lower = jnp.linalg.cholesky(gram)]
    another operation x1 -> x0, matrix products: 1.5 us -> none  [shards(): lax.linalg.triangular_solve(lower, reduced_products, left_side=True, lowe...]
    unnamed x9 -> x7, local copies, waits for them, and re-layouts: 2.18 us -> 3.6 us
  transfers between devices with their start and end apart: 2 -> 0, of which waited for: 0 -> 0; matrix products, arithmetic and copies ran while one was open for 5% -> 0% of each run, Pallas kernels for 0% -> 0%
where the time goes in v1:
time: 28.9 us; the launch traced here: 28.7 us
  Pallas kernels  24.4 us (84%)
  local copies, waits for them, and re-layouts  3.6 us (12%)
  between operations  0.65 us (2%)
    pallas_call x1, Pallas kernels, shards(): pl.pallas_call(functools.partial(step_kernel, n, planes, ny, planes * ny...  24.4 us
    unnamed x7, local copies, waits for them, and re-layouts  3.6 us

profile of v1, /device:TPU:0, one launch (start us, length us, event | category | flops | bytes accessed | tf_op | source)
XLA Modules:
  0.0 28.7 jit_solution(16954362129577577221)
XLA Ops:
  0.6 24.4 %shard_map.85 = (f32[16,128,128]{2,1,0:T(8,128)}, f32[16,16]{1,0:T(8,128)}, f32[16,16]{1,0:T(8,128)}) custom-call(f32[16,128,128]{2,1,0:T(8,128)} %bitcast.3, f32[16,128,128]{2,1,0:T(8,128)} %bitcast.4, s32[8,16,128]{2,1,0:T(8,128)} %reg_hbm.1, f32[8]{0:T(128)} %dens.1, f32[8]{0:T(128)} %stiff.1, f32[8]{0:T(128)} %dampt.1), custom_call_target="tpu_custom_call" | custom-call | tf_op jit(solution)/shard_map/pallas_call | solution.py:288
  25.1 0.0 copy-start.1
  25.1 2.3 %copy.12 = f32[16,8,16,128]{3,2,1,0:T(8,128)} copy(f32[16,8,16,128]{3,2,1,0:T(8,128)} %bitcast.5) | data formatting | bytes 2097152
  27.4 0.0 copy-done.1
  27.4 0.0 copy-start
  27.4 0.6 %copy.13 = f32[16,16]{1,0:T(8,128)} copy(f32[16,16]{1,0:T(8,128)S(1)} %copy-done.1) | data formatting | bytes 2048
  28.0 0.1 copy-done
  28.1 0.6 %copy.14 = f32[16,16]{1,0:T(8,128)} copy(f32[16,16]{1,0:T(8,128)S(1)} %copy-done) | data formatting | bytes 2048
Async XLA Ops:
  25.1 2.3 %copy-start.1 = (f32[16,16]{1,0:T(8,128)S(1)}, f32[16,16]{1,0:T(8,128)}, u32[]{:S(2)}) copy-start(f32[16,16]{1,0:T(8,128)} %get-tuple-element.13) | copy-start | bytes 3076
  27.4 0.7 %copy-start = (f32[16,16]{1,0:T(8,128)S(1)}, f32[16,16]{1,0:T(8,128)}, u32[]{:S(2)}) copy-start(f32[16,16]{1,0:T(8,128)} %get-tuple-element.14) | copy-start | bytes 3076

commit v2 on v1

--- a/solution.py
+++ b/solution.py
@@ -35,14 +35,14 @@
 def step_kernel(
     n, planes, ny, cells,
     b_hbm, c_hbm, reg_hbm, dens, stiff, dampt,
-    out_hbm, proj_ref, rfac_ref,
-    bv, cv, reg, coef, co, s, acc, ov, *rest,
+    s, w_ref, proj_ref, rfac_ref,
+    bv, cv, reg, coef, co, acc, *rest,
 ):
     rads = radices(n)
     slots = rest[: len(rads)]
-    load_sem, halo_send, halo_recv, reg_send, reg_recv, out_sem = rest[len(rads): len(rads) + 6]
-    ph_send = rest[len(rads) + 6: 2 * len(rads) + 6]
-    ph_recv = rest[2 * len(rads) + 6:]
+    load_sem, halo_send, halo_recv, reg_send, reg_recv = rest[len(rads): len(rads) + 5]
+    ph_send = rest[len(rads) + 5: 2 * len(rads) + 5]
+    ph_recv = rest[2 * len(rads) + 5:]
     k = b_hbm.shape[0]
     rows = planes * ny
     span = rows + 2 * ny
@@ -244,34 +244,43 @@
     rfac_ref[...] = jnp.where(ri <= ci, m[:, :k], 0.0)
 
     w = jnp.concatenate(split3(m[:, k:]), axis=0)
-    w = jnp.concatenate([w, w, w], axis=1)
-
+    w_ref[...] = jnp.concatenate([w, w, w], axis=1)
+
+    @pl.when(has_right)
+    def _():
+        for c in halo(True):
+            c.wait_send()
+
+    @pl.when(has_left)
+    def _():
+        for c in halo(False):
+            c.wait_send()
+
+
+def apply_kernel(planes, ny, s, w_ref, proj_in, rfac_in, out_hbm, proj_ref, rfac_ref, ov, out_sem):
+    k = proj_in.shape[0]
+    rows = planes * ny
+    nz = ov.shape[-1]
+    w = w_ref[...]
     ov3 = ov.reshape(k, rows, nz)
+
+    def send(x):
+        part = pl.ds(x * ny, ny)
+        return pltpu.make_async_copy(ov3.at[:, part, :], out_hbm.at[:, part, :], out_sem.at[x])
 
     def apply(x, _):
         o = jnp.dot(w, s[x], preferred_element_type=F32)
         o = o[:k] + (o[k: 2 * k] + o[2 * k:])
         for y in range(ny):
             ov[pl.ds(x * ny + y, k, stride=rows), :] = o[:, y * nz: (y + 1) * nz]
-        part = pl.ds(x * ny, ny)
-        pltpu.make_async_copy(ov3.at[:, part, :], out_hbm.at[:, part, :], out_sem.at[x]).start()
+        send(x).start()
         return 0
 
     lax.fori_loop(0, planes, apply, 0)
-
-    @pl.when(has_right)
-    def _():
-        for c in halo(True):
-            c.wait_send()
-
-    @pl.when(has_left)
-    def _():
-        for c in halo(False):
-            c.wait_send()
-
+    proj_ref[...] = proj_in[...]
+    rfac_ref[...] = rfac_in[...]
     for x in range(planes):
-        part = pl.ds(x * ny, ny)
-        pltpu.make_async_copy(ov3.at[:, part, :], out_hbm.at[:, part, :], out_sem.at[x]).wait()
+        send(x).wait()
 
 
 def solution(mesh):
@@ -282,27 +291,26 @@
         k, planes, ny, nz = b.shape
         rows = planes * ny
         tall = 2 * k * 2 * k // nz
-        hbm = pl.BlockSpec(memory_space=pl.ANY)
+        hbm = pl.BlockSpec(memory_space=pltpu.HBM)
         vm = pl.BlockSpec(memory_space=pltpu.VMEM)
         sm = pl.BlockSpec(memory_space=pltpu.SMEM)
-        new, proj, rfac = pl.pallas_call(
+        s, w, proj, rfac = pl.pallas_call(
             functools.partial(step_kernel, n, planes, ny, planes * ny * nz * n),
             out_shape=(
-                jax.ShapeDtypeStruct((k, rows, nz), F32),
-                jax.ShapeDtypeStruct((k, k), F32),
-                jax.ShapeDtypeStruct((k, k), F32),
+                pltpu.VMEM((planes, 6 * k, ny * nz), BF16),
+                pltpu.VMEM((3 * k, 6 * k), BF16),
+                pltpu.VMEM((k, k), F32),
+                pltpu.VMEM((k, k), F32),
             ),
             in_specs=[hbm, hbm, hbm, sm, sm, sm],
-            out_specs=(hbm, vm, vm),
+            out_specs=(vm, vm, vm, vm),
             scratch_shapes=[
                 pltpu.VMEM((k * (rows + 2 * ny), nz), F32),
                 pltpu.VMEM((k * rows, nz), F32),
                 pltpu.VMEM((planes + 2, ny, nz), jnp.int32),
                 pltpu.VMEM((planes + 2, ny, nz), F32),
                 pltpu.VMEM((8, ny, nz), F32),
-                pltpu.VMEM((planes, 6 * k, ny * nz), BF16),
                 pltpu.VMEM((6 * k, 6 * k), F32),
-                pltpu.VMEM((k * rows, nz), F32),
             ]
             + [pltpu.VMEM((r, tall, nz), F32) for r in rads]
             + [
@@ -311,12 +319,30 @@
                 pltpu.SemaphoreType.DMA((2,)),
                 pltpu.SemaphoreType.DMA((2,)),
                 pltpu.SemaphoreType.DMA((2,)),
-                pltpu.SemaphoreType.DMA((planes,)),
             ]
             + [pltpu.SemaphoreType.DMA((r,)) for r in rads]
             + [pltpu.SemaphoreType.DMA((r,)) for r in rads],
-            compiler_params=pltpu.CompilerParams(collective_id=0, has_side_effects=True),
+            compiler_params=pltpu.CompilerParams(
+                collective_id=0, has_side_effects=True, vmem_limit_bytes=60 << 20
+            ),
+            name="step",
         )(b.reshape(k, rows, nz), c.reshape(k, rows, nz), region, dens, stiff, dampt)
+        new, proj, rfac = pl.pallas_call(
+            functools.partial(apply_kernel, planes, ny),
+            out_shape=(
+                jax.ShapeDtypeStruct((k, rows, nz), F32),
+                jax.ShapeDtypeStruct((k, k), F32),
+                jax.ShapeDtypeStruct((k, k), F32),
+            ),
+            in_specs=[vm, vm, vm, vm],
+            out_specs=(hbm, vm, vm),
+            scratch_shapes=[
+                pltpu.VMEM((k * rows, nz), F32),
+                pltpu.SemaphoreType.DMA((planes,)),
+            ],
+            name="apply",
+            compiler_params=pltpu.CompilerParams(vmem_limit_bytes=16 << 20),
+        )(*(pltpu.with_memory_space_constraint(a, pltpu.VMEM) for a in (s, w, proj, rfac)))
         return new.reshape(b.shape), proj, rfac
 
     placed = (

time: 28.9 us -> 25.2 us (0.87)
  local copies, waits for them, and re-layouts: 3.6 us -> 0 us
    unnamed x7 -> x0, local copies, waits for them, and re-layouts: 3.6 us -> none
    pallas_call x1, Pallas kernels: 24.4 us -> 21.1 us  [shards(): pl.pallas_call(functools.partial(step_kernel, n, planes, ny, planes * ny...]
    pallas_call x0 -> x1, Pallas kernels: none -> 3.23 us  [shards(): pl.pallas_call(functools.partial(apply_kernel, planes, ny), out_shape=(ja...]
where the time goes in v2:
time: 25.2 us; the launch traced here: 25 us
  Pallas kernels  24.4 us (97%)
  between operations  0.64 us (3%)
    pallas_call x1, Pallas kernels, shards(): pl.pallas_call(functools.partial(step_kernel, n, planes, ny, planes * ny...  21.1 us
    pallas_call x1, Pallas kernels, shards(): pl.pallas_call(functools.partial(apply_kernel, planes, ny), out_shape=(ja...  3.23 us

profile of v2, /device:TPU:0, one launch (start us, length us, event | category | flops | bytes accessed | tf_op | source)
XLA Modules:
  0.0 25.0 jit_solution(11130047473615732555)
XLA Ops:
  0.6 21.1 %step.1 = (bf16[8,96,2048]{2,1,0:T(8,128)(2,1)S(1)}, bf16[48,96]{1,0:T(8,128)(2,1)S(1)}, f32[16,16]{1,0:T(8,128)S(1)}, f32[16,16]{1,0:T(8,128)S(1)}) custom-call(f32[16,128,128]{2,1,0:T(8,128)} %bitcast.3, f32[16,128,128]{2,1,0:T(8,128)} %bitcast.4, s32[8,16,128]{2,1,0:T(8,128)} %reg_hbm.1, f32[8]{0:T(128)} %dens.1, f32[8]{0:T(128)} %stiff.1, f32[8]{0:T(128)} %dampt.1), custom_call_target="tpu_custom_call" | custom-call | tf_op jit(solution)/shard_map/step/pallas_call | solution.py:297
  21.8 3.2 %apply.1 = (f32[16,128,128]{2,1,0:T(8,128)}, f32[16,16]{1,0:T(8,128)}, f32[16,16]{1,0:T(8,128)}) custom-call(bf16[8,96,2048]{2,1,0:T(8,128)(2,1)S(1)} %get-tuple-element.10.s, bf16[48,96]{1,0:T(8,128)(2,1)S(1)} %get-tuple-element.11.w_ref, f32[16,16]{1,0:T(8,128)S(1)} %get-tuple-element.12.proj_in, f32[16,16]{1,0:T(8,128)S(1)} %get-tuple-element.13.rfac_in), custom_call_target="tpu_custom_call" | custom-call | tf_op jit(solution)/shard_map/apply/pallas_call | solution.py:330

commit v3 on v2

--- a/solution.py
+++ b/solution.py
@@ -15,11 +15,8 @@
 def radices(count):
     out = []
     while count > 1:
-        for r in (8, 4, 2):
-            if count % r == 0:
-                break
-        else:
-            r = next(q for q in range(3, count + 1) if count % q == 0)
+        top = 16 if out else 2
+        r = next((q for q in range(top, 1, -1) if count % q == 0), count)
         out.append(r)
         count //= r
     return out
@@ -276,7 +273,7 @@
         send(x).start()
         return 0
 
-    lax.fori_loop(0, planes, apply, 0)
+    lax.fori_loop(0, planes, apply, 0, unroll=True)
     proj_ref[...] = proj_in[...]
     rfac_ref[...] = rfac_in[...]
     for x in range(planes):

time: 25.2 us -> 23.4 us (0.929)
  Pallas kernels: 24.4 us -> 22.6 us
    pallas_call x1, Pallas kernels: 3.23 us -> 2.2 us  [shards(): pl.pallas_call(functools.partial(apply_kernel, planes, ny), out_shape=(ja...]
    pallas_call x1, Pallas kernels: 21.1 us -> 20.4 us  [shards(): pl.pallas_call(functools.partial(step_kernel, n, planes, ny, planes * ny...]
where the time goes in v3:
time: 23.4 us; the launch traced here: 23.2 us
  Pallas kernels  22.6 us (97%)
  between operations  0.64 us (3%)
    pallas_call x1, Pallas kernels, shards(): pl.pallas_call(functools.partial(step_kernel, n, planes, ny, planes * ny...  20.4 us
    pallas_call x1, Pallas kernels, shards(): pl.pallas_call(functools.partial(apply_kernel, planes, ny), out_shape=(ja...  2.2 us

profile of v3, /device:TPU:0, one launch (start us, length us, event | category | flops | bytes accessed | tf_op | source)
XLA Modules:
  0.0 23.2 jit_solution(13587628177799251283)
XLA Ops:
  0.6 20.4 %step.1 = (bf16[8,96,2048]{2,1,0:T(8,128)(2,1)S(1)}, bf16[48,96]{1,0:T(8,128)(2,1)S(1)}, f32[16,16]{1,0:T(8,128)S(1)}, f32[16,16]{1,0:T(8,128)S(1)}) custom-call(f32[16,128,128]{2,1,0:T(8,128)} %bitcast.3, f32[16,128,128]{2,1,0:T(8,128)} %bitcast.4, s32[8,16,128]{2,1,0:T(8,128)} %reg_hbm.1, f32[8]{0:T(128)} %dens.1, f32[8]{0:T(128)} %stiff.1, f32[8]{0:T(128)} %dampt.1), custom_call_target="tpu_custom_call" | custom-call | tf_op jit(solution)/shard_map/step/pallas_call | solution.py:294
  21.0 2.2 %apply.1 = (f32[16,128,128]{2,1,0:T(8,128)}, f32[16,16]{1,0:T(8,128)}, f32[16,16]{1,0:T(8,128)}) custom-call(bf16[8,96,2048]{2,1,0:T(8,128)(2,1)S(1)} %get-tuple-element.10.s, bf16[48,96]{1,0:T(8,128)(2,1)S(1)} %get-tuple-element.11.w_ref, f32[16,16]{1,0:T(8,128)S(1)} %get-tuple-element.12.proj_in, f32[16,16]{1,0:T(8,128)S(1)} %get-tuple-element.13.rfac_in), custom_call_target="tpu_custom_call" | custom-call | tf_op jit(solution)/shard_map/apply/pallas_call | solution.py:327

commit v4 on v3

--- a/solution.py
+++ b/solution.py
@@ -33,7 +33,7 @@
     n, planes, ny, cells,
     b_hbm, c_hbm, reg_hbm, dens, stiff, dampt,
     s, w_ref, proj_ref, rfac_ref,
-    bv, cv, reg, coef, co, acc, *rest,
+    bv, cv, reg, coef, co, acc, fe, ready, *rest,
 ):
     rads = radices(n)
     slots = rest[: len(rads)]
@@ -59,6 +59,18 @@
         pd = lax.rem(d + o, rads[ph])
         return me + (pd - d) * st, pd
 
+    near, far = [], []
+    for r, (st, _) in zip(rads, digits):
+        inner = next((q for q in (4, 2) if r > 4 and r % q == 0), r)
+        near.append((st, inner))
+        if inner < r:
+            near.append((st * inner, r // inner))
+            far.append((st * inner, r // inner))
+
+    def members(st, r):
+        d = lax.rem(me // st, r)
+        return [me + (lax.rem(d + o, r) - d) * st for o in range(1, r)]
+
     barrier = pltpu.get_barrier_semaphore()
 
     @pl.when(has_left)
@@ -69,9 +81,11 @@
     def _():
         pl.semaphore_signal(barrier, inc=1, device_id=(right,), device_id_type=MESH)
 
-    for ph, r in enumerate(rads):
-        for o in range(1, r):
-            pl.semaphore_signal(barrier, inc=1, device_id=(peer(ph, o)[0],), device_id_type=MESH)
+    greeted = 0
+    for st, r in near:
+        for to in members(st, r):
+            pl.semaphore_signal(barrier, inc=1, device_id=(to,), device_id_type=MESH)
+            greeted += 1
 
     bv3 = bv.reshape(k, span, nz)
     cp_r = pltpu.make_async_copy(reg_hbm, reg.at[pl.ds(1, planes)], load_sem.at[0])
@@ -82,7 +96,7 @@
     cp_c.start()
 
     pl.semaphore_wait(
-        barrier, sum(r - 1 for r in rads) + has_left.astype(jnp.int32) + has_right.astype(jnp.int32)
+        barrier, greeted + has_left.astype(jnp.int32) + has_right.astype(jnp.int32)
     )
 
     def halo(up):
@@ -110,6 +124,10 @@
         for c in halo(False):
             c.start()
 
+    for i, (st, r) in enumerate(far):
+        for to in members(st, r):
+            pl.semaphore_signal(ready.at[i], inc=1, device_id=(to,), device_id_type=MESH)
+
     def lookup(r, table):
         out = jnp.zeros(r.shape, F32)
         for t in range(tables):
@@ -124,15 +142,18 @@
     lane = lax.broadcasted_iota(jnp.int32, (ny, nz), 1)
     acc[...] = jnp.zeros(acc.shape, F32)
 
-    def plane(x):
+    def plane(x, edge=None):
         c = coef[x + 1]
         r = reg[x + 1]
-        cxm, cxp = coef[x], coef[x + 2]
+        cxm = c if edge == 0 else coef[x]
+        cxp = c if edge == 1 else coef[x + 2]
         cym = jnp.concatenate([c[:1], c[:-1]], axis=0)
         cyp = jnp.concatenate([c[1:], c[-1:]], axis=0)
         czm = jnp.where(lane == 0, c, pltpu.roll(c, 1, 1))
         czp = jnp.where(lane == nz - 1, c, pltpu.roll(c, nz - 1, 1))
         bonds = [0.5 * (c + d) for d in (cxm, cxp, cym, cyp, czm, czp)]
+        if edge is not None:
+            bonds[edge] = jnp.zeros_like(c)
         co[0] = bonds[0] + bonds[1] + bonds[2] + bonds[3] + bonds[4] + bonds[5] - lookup(r, stiff)
         co[1] = lookup(r, dampt)
         for i in range(4):
@@ -148,19 +169,45 @@
             w = [jnp.broadcast_to(co[i, pl.ds(y, 1), :], (k, nz)) for i in range(8)]
             v = at(base + y)
             f = w[0] * v + w[1] * cv[pl.ds(x * ny + y, k, stride=rows), :]
-            f = f - w[2] * at(base + y - ny) - w[3] * at(base + y + ny)
+            if edge != 0:
+                f = f - w[2] * at(base + y - ny)
+            if edge != 1:
+                f = f - w[3] * at(base + y + ny)
             if y > 0:
                 f = f - w[4] * at(base + y - 1)
             if y < ny - 1:
                 f = f - w[5] * at(base + y + 1)
             f = f - w[6] * pltpu.roll(v, 1, 1) - w[7] * pltpu.roll(v, nz - 1, 1)
-            for i, (pb, pf) in enumerate(zip(split3(v), split3(f))):
+            for i, pb in enumerate(split3(v)):
                 s[x, pl.ds(2 * k * i, k), pl.ds(y * nz, nz)] = pb
-                s[x, pl.ds(2 * k * i + k, k), pl.ds(y * nz, nz)] = pf
+            if edge is None:
+                put(x, y, f)
+            else:
+                fe[edge, pl.ds(y * k, k), :] = f
+        if edge is None:
+            gram_of(x)
+
+    def put(x, y, f):
+        for i, pf in enumerate(split3(f)):
+            s[x, pl.ds(2 * k * i + k, k), pl.ds(y * nz, nz)] = pf
+
+    def finish(x, edge):
+        co[edge] = 0.5 * (coef[x + 1] + coef[x + 2 * edge])
+        row = (x + 1) * ny
+        halo_row = (x + 2 * edge) * ny
+        for y in range(ny):
+            w = jnp.broadcast_to(co[edge, pl.ds(y, 1), :], (k, nz))
+            v = bv[pl.ds(row + y, k, stride=span), :] - bv[pl.ds(halo_row + y, k, stride=span), :]
+            put(x, y, fe[edge, pl.ds(y * k, k), :] + w * v)
+        gram_of(x)
+
+    def gram_of(x):
         sx = s[x]
         acc[...] += lax.dot_general(sx, sx, (((1,), (1,)), ((), ())), preferred_element_type=F32)
 
-    lax.fori_loop(1, planes - 1, lambda x, _: (plane(x), 0)[1], 0)
+    lax.fori_loop(1, planes - 1, lambda x, _: (plane(x), 0)[1], 0, unroll=2)
+    plane(0, 0)
+    plane(planes - 1, 1)
 
     @pl.when(has_left)
     def _():
@@ -184,7 +231,8 @@
         bv3[:, pl.ds(rows + ny, ny), :] = jnp.zeros((k, ny, nz), F32)
         coef[planes + 1] = coef[planes]
 
-    lax.fori_loop(0, 2, lambda i, _: (plane(i * (planes - 1)), 0)[1], 0)
+    finish(0, 0)
+    finish(planes - 1, 1)
 
     g = acc[...]
     g = g[: 2 * k] + g[2 * k: 4 * k] + g[4 * k:]
@@ -192,6 +240,9 @@
     parts = nz // (2 * k)
     tall = (2 * k) // parts
     packed = jnp.concatenate([g[i * tall: (i + 1) * tall] for i in range(parts)], axis=1)
+
+    for i, (st, r) in enumerate(far):
+        pl.semaphore_wait(ready.at[i], r - 1)
 
     for ph, r in enumerate(rads):
         d = digits[ph][1]
@@ -308,6 +359,8 @@
                 pltpu.VMEM((planes + 2, ny, nz), F32),
                 pltpu.VMEM((8, ny, nz), F32),
                 pltpu.VMEM((6 * k, 6 * k), F32),
+                pltpu.VMEM((2, ny * k, nz), F32),
+                pltpu.SemaphoreType.REGULAR((len(rads),)),
             ]
             + [pltpu.VMEM((r, tall, nz), F32) for r in rads]
             + [

time: 23.4 us -> 22.8 us (0.974)
  Pallas kernels: 22.6 us -> 22 us
    pallas_call x1, Pallas kernels: 20.4 us -> 19.8 us  [shards(): pl.pallas_call(functools.partial(step_kernel, n, planes, ny, planes * ny...]
where the time goes in v4:
time: 22.8 us; the launch traced here: 22.6 us
  Pallas kernels  22 us (96%)
  between operations  0.64 us (3%)
    pallas_call x1, Pallas kernels, shards(): pl.pallas_call(functools.partial(step_kernel, n, planes, ny, planes * ny...  19.8 us
    pallas_call x1, Pallas kernels, shards(): pl.pallas_call(functools.partial(apply_kernel, planes, ny), out_shape=(ja...  2.2 us

profile of v4, /device:TPU:0, one launch (start us, length us, event | category | flops | bytes accessed | tf_op | source)
XLA Modules:
  0.0 22.6 jit_solution(2300102844700485640)
XLA Ops:
  0.6 19.8 %step.1 = (bf16[8,96,2048]{2,1,0:T(8,128)(2,1)S(1)}, bf16[48,96]{1,0:T(8,128)(2,1)S(1)}, f32[16,16]{1,0:T(8,128)S(1)}, f32[16,16]{1,0:T(8,128)S(1)}) custom-call(f32[16,128,128]{2,1,0:T(8,128)} %bitcast.3, f32[16,128,128]{2,1,0:T(8,128)} %bitcast.4, s32[8,16,128]{2,1,0:T(8,128)} %reg_hbm.1, f32[8]{0:T(128)} %dens.1, f32[8]{0:T(128)} %stiff.1, f32[8]{0:T(128)} %dampt.1), custom_call_target="tpu_custom_call" | custom-call | tf_op jit(solution)/shard_map/step/pallas_call | solution.py:345
  20.4 2.2 %apply.1 = (f32[16,128,128]{2,1,0:T(8,128)}, f32[16,16]{1,0:T(8,128)}, f32[16,16]{1,0:T(8,128)}) custom-call(bf16[8,96,2048]{2,1,0:T(8,128)(2,1)S(1)} %get-tuple-element.10.s, bf16[48,96]{1,0:T(8,128)(2,1)S(1)} %get-tuple-element.11.w_ref, f32[16,16]{1,0:T(8,128)S(1)} %get-tuple-element.12.proj_in, f32[16,16]{1,0:T(8,128)S(1)} %get-tuple-element.13.rfac_in), custom_call_target="tpu_custom_call" | custom-call | tf_op jit(solution)/shard_map/apply/pallas_call | solution.py:380

commit v5 on v4

--- a/solution.py
+++ b/solution.py
@@ -95,6 +95,14 @@
     cp_b.start()
     cp_c.start()
 
+    def lookup(r, table):
+        out = jnp.zeros(r.shape, F32)
+        for t in range(tables):
+            out = jnp.where(r == t, table[t], out)
+        return out
+
+    cp_r.wait()
+    coef[pl.ds(1, planes)] = lookup(reg[pl.ds(1, planes)], dens)
     pl.semaphore_wait(
         barrier, greeted + has_left.astype(jnp.int32) + has_right.astype(jnp.int32)
     )
@@ -128,14 +136,6 @@
         for to in members(st, r):
             pl.semaphore_signal(ready.at[i], inc=1, device_id=(to,), device_id_type=MESH)
 
-    def lookup(r, table):
-        out = jnp.zeros(r.shape, F32)
-        for t in range(tables):
-            out = jnp.where(r == t, table[t], out)
-        return out
-
-    cp_r.wait()
-    coef[pl.ds(1, planes)] = lookup(reg[pl.ds(1, planes)], dens)
     cp_b.wait()
     cp_c.wait()
 

time: 22.8 us -> 22.8 us (level)
  no operation moved by 1% of the time
where the time goes in v5:
time: 22.8 us; the launch traced here: 22.6 us
  Pallas kernels  22 us (96%)
  between operations  0.64 us (3%)
    pallas_call x1, Pallas kernels, shards(): pl.pallas_call(functools.partial(step_kernel, n, planes, ny, planes * ny...  19.8 us
    pallas_call x1, Pallas kernels, shards(): pl.pallas_call(functools.partial(apply_kernel, planes, ny), out_shape=(ja...  2.2 us

profile of v5, /device:TPU:0, one launch (start us, length us, event | category | flops | bytes accessed | tf_op | source)
XLA Modules:
  0.0 22.6 jit_solution(8525818973628851789)
XLA Ops:
  0.6 19.8 %step.1 = (bf16[8,96,2048]{2,1,0:T(8,128)(2,1)S(1)}, bf16[48,96]{1,0:T(8,128)(2,1)S(1)}, f32[16,16]{1,0:T(8,128)S(1)}, f32[16,16]{1,0:T(8,128)S(1)}) custom-call(f32[16,128,128]{2,1,0:T(8,128)} %bitcast.3, f32[16,128,128]{2,1,0:T(8,128)} %bitcast.4, s32[8,16,128]{2,1,0:T(8,128)} %reg_hbm.1, f32[8]{0:T(128)} %dens.1, f32[8]{0:T(128)} %stiff.1, f32[8]{0:T(128)} %dampt.1), custom_call_target="tpu_custom_call" | custom-call | tf_op jit(solution)/shard_map/step/pallas_call | solution.py:345
  20.4 2.2 %apply.1 = (f32[16,128,128]{2,1,0:T(8,128)}, f32[16,16]{1,0:T(8,128)}, f32[16,16]{1,0:T(8,128)}) custom-call(bf16[8,96,2048]{2,1,0:T(8,128)(2,1)S(1)} %get-tuple-element.10.s, bf16[48,96]{1,0:T(8,128)(2,1)S(1)} %get-tuple-element.11.w_ref, f32[16,16]{1,0:T(8,128)S(1)} %get-tuple-element.12.proj_in, f32[16,16]{1,0:T(8,128)S(1)} %get-tuple-element.13.rfac_in), custom_call_target="tpu_custom_call" | custom-call | tf_op jit(solution)/shard_map/apply/pallas_call | solution.py:380
